TPU v7x, 32 devices: a whole 2x2x4 slice. The times are simulated.
32 devices in a mesh: ctx: 4 (over y, x), exp: 8 (over z, core).
Axes of the slice: x: 2, y: 2, z: 4, core: 2. Of those that a mesh axis runs over, the one named last changes fastest.
Arguments:
- residual: bfloat16 [512, 4096], P('ctx'), may hold values from -4 to 4
- ssm_input: bfloat16 [512, 8192], P('ctx', 'exp'), may hold values from -16 to 16
- ssm_gate: bfloat16 [512, 8192], P('ctx', 'exp'), may hold values from -5 to 5
- write_vectors: bfloat16 [512, 128], P('ctx'), may hold values from -1.75 to 1.75
- read_vectors: bfloat16 [512, 128], P('ctx'), may hold values from -1.75 to 1.75
- step_logits: float32 [128, 512], P('exp', 'ctx'), may hold values from -2 to 1536
- decay_log: float32 [128], P('exp'), may hold values from -12 to -2
- skip_gain: float32 [128], P('exp'), may hold values from 0.5 to 3
- norm_gain: float32 [8192], P('exp'), may hold values from 0.1 to 1.9
- out_weight: bfloat16 [8192, 4096], P('exp', 'ctx'), may hold values from -0.09375 to 0.09375
- moe_gain: float32 [4096], replicated, may hold values from 0.1 to 1.9
- gate_weight: bfloat16 [8, 4096, 12288], P('exp', None, 'ctx'), may hold values from -0.09375 to 0.09375
- up_weight: bfloat16 [8, 4096, 12288], P('exp', None, 'ctx'), may hold values from -0.09375 to 0.09375
- down_weight: bfloat16 [8, 12288, 4096], P('exp', 'ctx'), may hold values from -0.0546875 to 0.0546875
- expert_ids: int32 [512, 2], P('ctx'), may hold values from 0 to 7, all different within a row; in each aligned block of 128 rows (0 to 127, 128 to 255, ...) at most 64 rows name the same one
- route_weight: float32 [512, 2], P('ctx'), may hold values from 0.5 to 1.5
Outputs:
- layer_out: bfloat16 [512, 4096], P('ctx', 'exp')
Inputs may be any that keep to these rules, and one draw needn't show every extreme that they name: `expert_ids`: each row names 2 different experts. Among the 128 rows of one index of ctx no expert is named by more than 64 rows, and in every draw some expert is named by exactly 64 of them.
All inputs are finite; a program needn't handle non-finite values.
Results may differ from a plain program's by a relative error of at most 0.023.
Values may be sent and summed in bfloat16 or wider, within the bound.
A program may use at most 192 MiB of HBM per device.

v0:
```python
import jax
import jax.numpy as jnp
from jax import lax
from jax.sharding import PartitionSpec as P

SPAN = 128
NORM_GROUP = 512
EXPERTS = 8
CAP = 64
EPSILON = 1e-05


def passed_along(block, axis, distance):
    devices = range(lax.axis_size(axis))
    route = [(i - distance, i) for i in devices if i - distance in devices]
    return lax.ppermute(block, axis, route)


def slot_tables(block_ids):
    expert_range = jnp.arange(EXPERTS, dtype=jnp.int32)
    hit_table = jnp.sum(
        (block_ids[:, :, None] == expert_range[None, None, :]).astype(jnp.int32), axis=1
    )
    ranking = jnp.cumsum(hit_table, axis=0) - 1
    slot_range = jnp.arange(CAP, dtype=jnp.int32)
    matches = (hit_table.T[:, None, :] == 1) & (ranking.T[:, None, :] == slot_range[None, :, None])
    row_count = block_ids.shape[0]
    row_range = jnp.arange(row_count, dtype=jnp.int32)
    chosen = jnp.sum(jnp.where(matches, row_range[None, None, :], 0), axis=2)
    filled = jnp.any(matches, axis=2)
    token_of_slot = jnp.where(filled, chosen, row_count)
    pick_rank = jnp.take_along_axis(ranking, block_ids, axis=1)
    return (token_of_slot, pick_rank)


def normalize(stream_rows, moe_gain):
    values = stream_rows.astype(jnp.float32)
    scale_inv = lax.rsqrt(jnp.mean(values * values, axis=-1, keepdims=True) + EPSILON)
    return (values * scale_inv * moe_gain).astype(jnp.bfloat16)


def body(
    residual,
    ssm_input,
    ssm_gate,
    write_vectors,
    read_vectors,
    step_logits,
    decay_log,
    skip_gain,
    norm_gain,
    out_weight,
    moe_gain,
    gate_weight,
    up_weight,
    down_weight,
    expert_ids,
    route_weight,
):
    heads_dev = step_logits.shape[0]
    tok_rows = step_logits.shape[1]
    head_width = ssm_input.shape[1] // heads_dev
    span_count = tok_rows // SPAN
    step_size = jax.nn.softplus(step_logits)
    log_step = step_size * (-jnp.exp(decay_log))[:, None]
    cumulative = jnp.cumsum(log_step.reshape(heads_dev, span_count, SPAN), axis=2)
    step_blocks = step_size.reshape(heads_dev, span_count, SPAN)
    input_blocks = ssm_input.reshape(span_count, SPAN, heads_dev, head_width)
    write_blocks = write_vectors.reshape(span_count, SPAN, -1)
    read_blocks = read_vectors.reshape(span_count, SPAN, -1)
    scores = jnp.einsum(
        "ktn,ksn->kts", read_blocks, write_blocks, preferred_element_type=jnp.float32
    )
    causal = jnp.arange(SPAN)[:, None] >= jnp.arange(SPAN)[None, :]
    log_gaps = cumulative[:, :, :, None] - cumulative[:, :, None, :]
    mixing = jnp.where(
        causal,
        scores[None] * jnp.exp(jnp.where(causal, log_gaps, 0.0)) * step_blocks[:, :, None, :],
        0.0,
    ).astype(jnp.bfloat16)
    intra_out = jnp.einsum(
        "hkts,kshp->kthp", mixing, input_blocks, preferred_element_type=jnp.float32
    )
    end_weight = jnp.exp(cumulative[:, :, -1:] - cumulative) * step_blocks
    loaded = (end_weight[:, :, :, None] * write_blocks.astype(jnp.float32)[None]).astype(
        jnp.bfloat16
    )
    block_state = jnp.einsum(
        "kshp,hksn->hkpn", input_blocks, loaded, preferred_element_type=jnp.float32
    )
    block_decay = jnp.exp(cumulative[:, :, -1])
    running = jnp.zeros_like(block_state[:, 0])
    decay_run = jnp.ones_like(block_decay[:, 0])
    entering_list = [running]
    reach_list = [decay_run]
    running = block_decay[:, 0, None, None] * running + block_state[:, 0]
    decay_run = decay_run * block_decay[:, 0]
    device_state = running
    device_decay = decay_run

    def forward(turn_index, incoming):
        return passed_along(
            (device_decay[:, None, None] * incoming + device_state).astype(jnp.bfloat16), "ctx", 1
        ).astype(jnp.float32)

    device_in = lax.fori_loop(0, lax.axis_size("ctx") - 1, forward, jnp.zeros_like(device_state))
    entering = jnp.stack(entering_list, axis=1)
    reach = jnp.stack(reach_list, axis=1)
    states = entering + reach[:, :, None, None] * device_in[:, None]
    inter_out = jnp.transpose(jnp.exp(cumulative), (1, 2, 0))[:, :, :, None] * jnp.einsum(
        "ktn,hkpn->kthp", read_blocks.astype(jnp.float32), states, precision=lax.Precision.HIGHEST
    )
    scan_out = (
        intra_out + inter_out + skip_gain[None, None, :, None] * input_blocks.astype(jnp.float32)
    )
    scan_out = scan_out.reshape(tok_rows, heads_dev * head_width)
    gated_out = scan_out * jax.nn.silu(ssm_gate.astype(jnp.float32))
    grouped = gated_out.reshape(tok_rows, -1, NORM_GROUP)
    group_scale = lax.rsqrt(jnp.mean(grouped * grouped, axis=2, keepdims=True) + EPSILON)
    normed = ((grouped * group_scale).reshape(tok_rows, -1) * norm_gain).astype(jnp.bfloat16)
    ssm_terms = jnp.dot(
        normed,
        lax.all_gather(out_weight, "ctx", axis=1, tiled=True),
        preferred_element_type=jnp.float32,
    )
    exp_count = lax.axis_size("exp")
    exp_index = lax.axis_index("exp")
    slice_width = residual.shape[1] // exp_count
    split_count = exp_count // EXPERTS
    own_residual = lax.dynamic_slice_in_dim(residual, exp_index * slice_width, slice_width, 1)
    ssm_sum = lax.psum(ssm_terms.astype(jnp.bfloat16), "exp").astype(jnp.float32)
    ssm_share = lax.dynamic_slice_in_dim(ssm_sum, exp_index * slice_width, slice_width, 1)
    stream_slice = (own_residual.astype(jnp.float32) + ssm_share).astype(jnp.bfloat16)
    token_of_slot, pick_rank = slot_tables(expert_ids)
    stream_full = lax.all_gather(stream_slice, "exp", axis=1, tiled=True)
    padded = jnp.concatenate(
        [stream_full, jnp.zeros((1, stream_full.shape[1]), jnp.bfloat16)], axis=0
    )
    my_slots = lax.dynamic_index_in_dim(token_of_slot, exp_index // split_count, 0, keepdims=False)
    picked = normalize(jnp.take(padded, my_slots, axis=0), moe_gain)
    normed_rows = lax.all_gather(picked, "ctx", axis=0, tiled=True)
    gate_val = jnp.dot(normed_rows, gate_weight[0], preferred_element_type=jnp.float32)
    up_val = jnp.dot(normed_rows, up_weight[0], preferred_element_type=jnp.float32)
    hidden = (jax.nn.silu(gate_val) * up_val).astype(jnp.bfloat16)
    sums_mine = lax.psum_scatter(
        jnp.dot(hidden, down_weight[0], preferred_element_type=jnp.float32).astype(jnp.bfloat16),
        "ctx",
        scatter_dimension=0,
        tiled=True,
    ).astype(jnp.float32)
    arrived = lax.all_to_all(
        sums_mine.astype(jnp.bfloat16), "exp", split_axis=1, concat_axis=0, tiled=True
    ).astype(sums_mine.dtype)
    piece_expert = jnp.arange(exp_count, dtype=jnp.int32) // split_count
    hit_expert = (expert_ids[:, :, None] == piece_expert[None, None, :]).astype(jnp.float32)
    hit_slot = (pick_rank[:, :, None] == jnp.arange(CAP, dtype=jnp.int32)[None, None, :]).astype(
        jnp.float32
    )
    combine_table = jnp.sum(
        route_weight[:, :, None, None] * hit_expert[:, :, :, None] * hit_slot[:, :, None, :], axis=1
    )
    combine_table = combine_table.reshape(tok_rows, exp_count * CAP)
    moe_slice = jnp.dot(
        combine_table, arrived, precision=lax.Precision.HIGHEST, preferred_element_type=jnp.float32
    )
    return (stream_slice.astype(jnp.float32) + moe_slice).astype(jnp.bfloat16)


def solution(mesh):
    placed = (
        P("ctx", None),
        P("ctx", "exp"),
        P("ctx", "exp"),
        P("ctx", None),
        P("ctx", None),
        P("exp", "ctx"),
        P("exp"),
        P("exp"),
        P("exp"),
        P("exp", "ctx"),
        P(),
        P("exp", None, "ctx"),
        P("exp", None, "ctx"),
        P("exp", "ctx", None),
        P("ctx", None),
        P("ctx", None),
    )
    return jax.shard_map(
        body, mesh=mesh, in_specs=placed, out_specs=P("ctx", "exp"), check_vma=False
    )
```

profile of v0, /device:TPU:0, one launch (start us, length us, event | category | flops | bytes accessed | tf_op | source)
XLA Modules:
  0.0 343.4 jit_solution(16639426668395161547)
XLA Ops:
  6.5 0.0 all-gather.4.cloned.1.call-start
  6.6 0.7 all-gather.4.cloned.1.call-update
  7.3 0.0 all-reduce.3.cloned.1.call-start
  7.3 1.1 copy.60
  8.5 1.1 copy.61
  9.6 0.1 compare_select_fusion
  9.7 0.3 reduce_window_sum.22
  10.0 0.2 multiply_reduce_fusion.1
  10.2 0.1 exponential_multiply_fusion
  10.3 0.5 fusion.27
  10.9 42.7 %while.11 = (s32[]{:T(128)}, f32[16,64,128]{2,1,0:T(8,128)S(1)}, f32[16,1]{0,1:T(1,128)S(1)}, f32[16,64,128]{2,1,0:T(8,128)S(1)}, s32[]{:T(128)}, /*index=5*/s32[]{:T(128)}) while((s32[]{:T(128)}, f32[16,64,128]{2,1,0:T(8,128)S(1)}, f32[16,1]{0,1:T(1,128)S(1)}, f32[16,64,128]{2,1,0:T(8,128)S(1)}, s32[]{:T(128)}, ...), condition=%wide.region_2.3_spmd.clone, body=%wide.region_1.2_spmd.clone.sunk | while | flops 655363 | bytes 3145911 | solution.py:106
  10.9 0.1 fusion.72
  11.0 4.9 %collective-permute-start = (bf16[16,64,128]{2,1,0:T(8,128)(2,1)S(1)}, bf16[16,64,128]{2,1,0:T(8,128)(2,1)S(1)}, u32[]{:S(2)}, u32[]{:S(2)}) collective-permute-start(bf16[16,64,128]{2,1,0:T(8,128)(2,1)S(1)} %fusion.72), channel_id=1, source_target_pairs={{0,8},{8,16},{16,24},{1,9},{9,17},{17,25},{2,10},{10,18},{18,26},{... | collective-permute-start | bytes 786440 | tf_op jit(solution)/shard_map/while/body/eval_jaxpr/ppermute | solution.py:16
  15.9 5.5 %collective-permute-done = bf16[16,64,128]{2,1,0:T(8,128)(2,1)S(1)} collective-permute-done((bf16[16,64,128]{2,1,0:T(8,128)(2,1)S(1)}, bf16[16,64,128]{2,1,0:T(8,128)(2,1)S(1)}, u32[]{:S(2)}, u32[]{:S(2)}) %collective-permute-start) | collective-permute-done | bytes 262176 | tf_op jit(solution)/shard_map/while/body/eval_jaxpr/ppermute | solution.py:16
  21.5 0.1 fusion.72
  21.6 4.4 %collective-permute-start = (bf16[16,64,128]{2,1,0:T(8,128)(2,1)S(1)}, bf16[16,64,128]{2,1,0:T(8,128)(2,1)S(1)}, u32[]{:S(2)}, u32[]{:S(2)}) collective-permute-start(bf16[16,64,128]{2,1,0:T(8,128)(2,1)S(1)} %fusion.72), channel_id=1, source_target_pairs={{0,8},{8,16},{16,24},{1,9},{9,17},{17,25},{2,10},{10,18},{18,26},{... | collective-permute-start | bytes 786440 | tf_op jit(solution)/shard_map/while/body/eval_jaxpr/ppermute | solution.py:16
  26.0 11.6 %collective-permute-done = bf16[16,64,128]{2,1,0:T(8,128)(2,1)S(1)} collective-permute-done((bf16[16,64,128]{2,1,0:T(8,128)(2,1)S(1)}, bf16[16,64,128]{2,1,0:T(8,128)(2,1)S(1)}, u32[]{:S(2)}, u32[]{:S(2)}) %collective-permute-start) | collective-permute-done | bytes 262176 | tf_op jit(solution)/shard_map/while/body/eval_jaxpr/ppermute | solution.py:16
  37.6 0.1 fusion.72
  37.8 4.4 %collective-permute-start = (bf16[16,64,128]{2,1,0:T(8,128)(2,1)S(1)}, bf16[16,64,128]{2,1,0:T(8,128)(2,1)S(1)}, u32[]{:S(2)}, u32[]{:S(2)}) collective-permute-start(bf16[16,64,128]{2,1,0:T(8,128)(2,1)S(1)} %fusion.72), channel_id=1, source_target_pairs={{0,8},{8,16},{16,24},{1,9},{9,17},{17,25},{2,10},{10,18},{18,26},{... | collective-permute-start | bytes 786440 | tf_op jit(solution)/shard_map/while/body/eval_jaxpr/ppermute | solution.py:16
  42.2 11.3 %collective-permute-done = bf16[16,64,128]{2,1,0:T(8,128)(2,1)S(1)} collective-permute-done((bf16[16,64,128]{2,1,0:T(8,128)(2,1)S(1)}, bf16[16,64,128]{2,1,0:T(8,128)(2,1)S(1)}, u32[]{:S(2)}, u32[]{:S(2)}) %collective-permute-start) | collective-permute-done | bytes 262176 | tf_op jit(solution)/shard_map/while/body/eval_jaxpr/ppermute | solution.py:16
  53.6 0.4 fusion.26
  54.0 0.1 fusion.61
  54.1 0.6 fusion.29
  54.7 0.0 copy-start.10
  54.7 0.2 copy.62
  54.9 0.2 fusion.60
  55.1 0.4 mul.209
  55.5 0.2 reduce_sum.45
  55.8 0.2 mul.210
  56.0 0.1 copy.71
  56.1 54.2 %all-gather.4.cloned.1.call-done = bf16[1024,4096]{1,0:T(8,128)(2,1)} async-done(((bf16[1024,1024]{1,0:T(8,128)(2,1)}), bf16[1024,4096]{1,0:T(8,128)(2,1)}) %all-gather.4.cloned.1.call-update) | async-done | bytes 8388624 | tf_op jit(solution)/shard_map/all_gather | solution.py:123
  110.3 5.8 %convolution_convert_fusion = bf16[128,4096]{1,0:T(8,128)(2,1)} fusion(bf16[1024,4096]{1,0:T(8,128)(2,1)} %all-gather.4.cloned.1.call-done, f32[128,1024]{1,0:T(8,128)S(1)} %bitcast.99, f32[1024]{0:T(1024)S(1)} %copy-done.10, f32[128,1024]{1,0:T(8,128)S(1)} %copy.62, bf16[128,1024]{1,0:T(8,128)(2,1)S(1)} %copy-done.3), kind=kOutput, calls=%fused_computation.12 | convolution fusion | flops 1075445760 | bytes 10752000 | tf_op jit(solution)/shard_map/dot_general | solution.py:121
  116.1 0.0 all-reduce.3.cloned.1.call-update
  116.2 0.0 all-gather.6.cloned.1.call-start
  116.2 58.9 %all-reduce.3.cloned.1.call-done = bf16[128,4096]{1,0:T(8,128)(2,1)} async-done(((bf16[128,4096]{1,0:T(8,128)(2,1)}), bf16[128,4096]{1,0:T(8,128)(2,1)}) %all-reduce.3.cloned.1.call-update) | async-done | bytes 1048592 | tf_op jit(solution)/shard_map/psum | solution.py:131
  175.1 1.7 add_convert_fusion
  176.8 0.0 all-gather.6.cloned.1.call-update
  176.8 0.0 all-gather.8.cloned.1.call-start
  176.9 0.1 copy.65
  177.0 0.2 reduce_window_sum.23
  177.2 0.2 fusion.50
  177.5 0.2 select_reduce_fusion
  177.8 20.3 %all-gather.6.cloned.1.call-done = bf16[128,4096]{1,0:T(8,128)(2,1)} async-done(((bf16[128,512]{1,0:T(8,128)(2,1)}), bf16[128,4096]{1,0:T(8,128)(2,1)}) %all-gather.6.cloned.1.call-update) | async-done | bytes 1048592 | tf_op jit(solution)/shard_map/all_gather | solution.py:135
  198.0 1.3 concatenate.3
  199.4 0.9 gather_fusion
  200.2 0.3 fusion.32
  200.6 1.0 fusion.34
  201.6 0.0 all-gather.8.cloned.1.call-update
  201.6 0.2 reduce-scatter.2.cloned.1.call-start
  201.8 34.9 %all-gather.8.cloned.1.call-done = bf16[256,4096]{1,0:T(8,128)(2,1)} async-done(((bf16[64,4096]{1,0:T(8,128)(2,1)}), bf16[256,4096]{1,0:T(8,128)(2,1)}) %all-gather.8.cloned.1.call-update) | async-done | bytes 2097168 | tf_op jit(solution)/shard_map/all_gather | solution.py:141
  236.7 16.7 %fusion.6 = f32[256,3072]{1,0:T(8,128)} fusion(bf16[256,4096]{1,0:T(8,128)(2,1)} %all-gather.8.cloned.1.call-done, bf16[1,4096,3072]{2,1,0:T(8,128)(2,1)} %param.29), kind=kOutput, calls=%fused_computation.9 | convolution fusion | flops 6442450944 | bytes 30408704 | tf_op jit(solution)/shard_map/dot_general | solution.py:142
  253.4 25.1 %fusion.8 = bf16[256,4096]{1,0:T(8,128)(2,1)} fusion(bf16[1,3072,4096]{2,1,0:T(8,128)(2,1)} %param.31, bf16[256,4096]{1,0:T(8,128)(2,1)S(1)} %copy-done.9, bf16[1,4096,3072]{2,1,0:T(8,128)(2,1)} %param.30, f32[256,3072]{1,0:T(8,128)} %fusion.6), kind=kOutput, calls=%fused_computation.11 | convolution fusion | flops 12890669056 | bytes 57671680 | tf_op jit(solution)/shard_map/dot_general | solution.py:146
  278.5 0.0 reduce-scatter.2.cloned.1.call-update
  278.5 35.4 %reduce-scatter.2.cloned.1.call-done = bf16[64,4096]{1,0:T(8,128)(2,1)} async-done(((bf16[256,4096]{1,0:T(8,128)(2,1)}), bf16[64,4096]{1,0:T(8,128)(2,1)}) %reduce-scatter.2.cloned.1.call-update) | async-done | bytes 524304 | tf_op jit(solution)/shard_map/reduce_scatter | solution.py:145
  313.9 1.9 copy.74
  315.8 4.6 %all-to-all-start = ((bf16[64,8,512]{2,0,1:T(8,128)(2,1)}), bf16[64,8,512]{2,0,1:T(8,128)(2,1)S(1)}, u32[]{:S(2)}, u32[]{:S(2)}) async-start(bf16[64,8,512]{2,0,1:T(8,128)(2,1)} %bitcast.90), calls=%async_computation.1 | async-start | bytes 1048576 | tf_op jit(solution)/shard_map/all_to_all | solution.py:151
  320.4 0.1 copy.66
  320.5 0.1 reshape.219
  320.7 1.9 gather_fusion.1
  322.6 0.1 reshape.222
  322.8 0.1 copy.67
  322.9 0.0 copy-done.8
  323.0 12.8 %all-to-all-done = bf16[64,8,512]{2,0,1:T(8,128)(2,1)S(1)} async-done(((bf16[64,8,512]{2,0,1:T(8,128)(2,1)}), bf16[64,8,512]{2,0,1:T(8,128)(2,1)S(1)}, u32[]{:S(2)}, u32[]{:S(2)}) %all-to-all-start) | async-done | bytes 524320 | tf_op jit(solution)/shard_map/all_to_all | solution.py:151
  335.8 1.1 fusion.31
  (47 shorter events, 0.4 us)
Async XLA Ops:
  6.5 47.1 %copy-start = (bf16[128,128]{1,0:T(8,128)(2,1)S(1)}, bf16[128,128]{1,0:T(8,128)(2,1)}, u32[]{:S(2)}) copy-start(bf16[128,128]{1,0:T(8,128)(2,1)} %param.22) | copy-start | bytes 98308
  6.5 3.0 copy-start.4
  6.5 3.0 copy-start.11
  6.5 3.1 copy-start.5
  6.5 103.8 %all-gather.4.cloned.1.call-start = ((), (), s32[]{:S(2)}) async-start(), calls=%async_computation.2 | async-start | bytes 10485760 | tf_op jit(solution)/shard_map/all_gather | solution.py:123
  7.3 167.9 %all-reduce.3.cloned.1.call-start = ((), (), s32[]{:S(2)}) async-start(), calls=%async_computation.3 | async-start | bytes 2097152 | tf_op jit(solution)/shard_map/psum | solution.py:131
  10.8 43.3 %copy-start.12 = (f32[16]{0:T(128)S(1)}, f32[16]{0:T(128)}, u32[]{:S(2)}) copy-start(f32[16]{0:T(128)} %param.25) | copy-start | bytes 196
  11.0 10.4 %collective-permute-start = (bf16[16,64,128]{2,1,0:T(8,128)(2,1)S(1)}, bf16[16,64,128]{2,1,0:T(8,128)(2,1)S(1)}, u32[]{:S(2)}, u32[]{:S(2)}) collective-permute-start(bf16[16,64,128]{2,1,0:T(8,128)(2,1)S(1)} %fusion.72), channel_id=1, source_target_pairs={{0,8},{8,16},{16,24},{1,9},{9,17},{17,25},{2,10},{10,18},{18,26},{... | collective-permute-start | bytes 786440 | tf_op jit(solution)/shard_map/while/body/eval_jaxpr/ppermute | solution.py:16
  21.6 16.0 %collective-permute-start = (bf16[16,64,128]{2,1,0:T(8,128)(2,1)S(1)}, bf16[16,64,128]{2,1,0:T(8,128)(2,1)S(1)}, u32[]{:S(2)}, u32[]{:S(2)}) collective-permute-start(bf16[16,64,128]{2,1,0:T(8,128)(2,1)S(1)} %fusion.72), channel_id=1, source_target_pairs={{0,8},{8,16},{16,24},{1,9},{9,17},{17,25},{2,10},{10,18},{18,26},{... | collective-permute-start | bytes 786440 | tf_op jit(solution)/shard_map/while/body/eval_jaxpr/ppermute | solution.py:16
  37.8 15.7 %collective-permute-start = (bf16[16,64,128]{2,1,0:T(8,128)(2,1)S(1)}, bf16[16,64,128]{2,1,0:T(8,128)(2,1)S(1)}, u32[]{:S(2)}, u32[]{:S(2)}) collective-permute-start(bf16[16,64,128]{2,1,0:T(8,128)(2,1)S(1)} %fusion.72), channel_id=1, source_target_pairs={{0,8},{8,16},{16,24},{1,9},{9,17},{17,25},{2,10},{10,18},{18,26},{... | collective-permute-start | bytes 786440 | tf_op jit(solution)/shard_map/while/body/eval_jaxpr/ppermute | solution.py:16
  53.6 1.3 copy-start.3
  54.7 55.6 %copy-start.10 = (f32[1024]{0:T(1024)S(1)}, f32[1024]{0:T(1024)}, u32[]{:S(2)}) copy-start(f32[1024]{0:T(1024)} %param.26) | copy-start | bytes 12292
  110.3 66.5 %copy-start.7 = (s32[128,2]{0,1:T(2,128)S(1)}, s32[128,2]{0,1:T(2,128)}, u32[]{:S(2)}) copy-start(s32[128,2]{0,1:T(2,128)} %param.32) | copy-start | bytes 3076
  116.2 81.8 %all-gather.6.cloned.1.call-start = ((), (), s32[]{:S(2)}) async-start(), calls=%async_computation.4 | async-start | bytes 1179648 | tf_op jit(solution)/shard_map/all_gather | solution.py:135
  176.8 59.9 %all-gather.8.cloned.1.call-start = ((), (), s32[]{:S(2)}) async-start(), calls=%async_computation.5 | async-start | bytes 2621440 | tf_op jit(solution)/shard_map/all_gather | solution.py:141
  199.4 1.2 copy-start.6
  201.6 112.3 %reduce-scatter.2.cloned.1.call-start = ((), (), s32[]{:S(2)}) async-start(), calls=%async_computation.6 | async-start | bytes 2621440 | tf_op jit(solution)/shard_map/reduce_scatter | solution.py:145
  236.7 16.7 %copy-start.9 = (bf16[256,4096]{1,0:T(8,128)(2,1)S(1)}, bf16[256,4096]{1,0:T(8,128)(2,1)}, u32[]{:S(2)}) copy-start(bf16[256,4096]{1,0:T(8,128)(2,1)} %all-gather.8.cloned.1.call-done) | copy-start | bytes 6291460
  315.8 20.0 %all-to-all-start = ((bf16[64,8,512]{2,0,1:T(8,128)(2,1)}), bf16[64,8,512]{2,0,1:T(8,128)(2,1)S(1)}, u32[]{:S(2)}, u32[]{:S(2)}) async-start(bf16[64,8,512]{2,0,1:T(8,128)(2,1)} %bitcast.90), calls=%async_computation.1 | async-start | bytes 1048576 | tf_op jit(solution)/shard_map/all_to_all | solution.py:151
  320.7 2.2 copy-start.8
  320.7 15.1 %copy-start.2 = (bf16[128,512]{1,0:T(8,128)(2,1)S(1)}, bf16[128,512]{1,0:T(8,128)(2,1)}, u32[]{:S(2)}) copy-start(bf16[128,512]{1,0:T(8,128)(2,1)} %add_convert_fusion) | copy-start | bytes 393220
  320.7 16.2 %copy-start.1 = (bf16[128,128]{1,0:T(8,128)(2,1)S(1)}, bf16[128,128]{1,0:T(8,128)(2,1)}, u32[]{:S(2)}) copy-start(bf16[128,128]{1,0:T(8,128)(2,1)} %param.22) | copy-start | bytes 98308
Sparse Core Ops, SparseCore 0:
  9.2 101.0 all-gather.3
  116.3 58.7 all-reduce.2
  176.9 21.0 all-gather.5
  201.7 34.9 all-gather.7
  278.7 35.1 reduce-scatter.1
where the time goes:
time: 344 us; the launch traced here: 343 us
  waiting for transfers between devices  246 us (72%)
  matrix products  50.4 us (15%)
  starting transfers between devices  18.6 us (5%)
  between operations  13.5 us (4%)
  local copies, waits for them, and re-layouts  9.85 us (3%)
  other arithmetic  5.34 us (2%)
    psum x1, waiting for transfers between devices, body(): lax.psum(ssm_terms.astype(jnp.bfloat16), 'exp').astype(jnp.float32)  58.9 us
    all_gather x1, waiting for transfers between devices, body(): lax.all_gather(out_weight, 'ctx', axis=1, tiled=True)  54.2 us
    reduce_scatter x1, waiting for transfers between devices, body(): lax.psum_scatter(jnp.dot(hidden, down_weight[0], preferred_element_type=j...  35.4 us
    all_gather x1, waiting for transfers between devices, body(): normed_rows = lax.all_gather(picked, 'ctx', axis=0, tiled=True)  34.9 us
    ppermute x3, waiting for transfers between devices, passed_along(): return lax.ppermute(block, axis, route)  28.4 us
    dot_general x1, matrix products, body(): jnp.dot(hidden, down_weight[0], preferred_element_type=jnp.float32)  25.1 us
    all_gather x1, waiting for transfers between devices, body(): stream_full = lax.all_gather(stream_slice, 'exp', axis=1, tiled=True)  20.3 us
    dot_general x1, matrix products, body(): jnp.dot(normed_rows, gate_weight[0], preferred_element_type=jnp.float32)  16.7 us
  transfers between devices with their start and end apart: 9, of which 9 were waited for; matrix products, arithmetic and copies ran while one was open for 3% of the time, Pallas kernels for 0%

commit v1 on v0

--- a/solution.py
+++ b/solution.py
@@ -128,7 +128,9 @@
     slice_width = residual.shape[1] // exp_count
     split_count = exp_count // EXPERTS
     own_residual = lax.dynamic_slice_in_dim(residual, exp_index * slice_width, slice_width, 1)
-    ssm_sum = lax.psum(ssm_terms.astype(jnp.bfloat16), "exp").astype(jnp.float32)
+    ssm_sum = jnp.sum(lax.all_gather(ssm_terms.astype(jnp.bfloat16), "exp"), axis=0).astype(
+        jnp.float32
+    )
     ssm_share = lax.dynamic_slice_in_dim(ssm_sum, exp_index * slice_width, slice_width, 1)
     stream_slice = (own_residual.astype(jnp.float32) + ssm_share).astype(jnp.bfloat16)
     token_of_slot, pick_rank = slot_tables(expert_ids)

time: 344 us -> 372 us (1.081)
  waiting for transfers between devices: 246 us -> 268 us
  other arithmetic: 5.34 us -> 10.2 us
    all_gather x0 -> x1, waiting for transfers between devices: none -> 82.2 us  [body(): lax.all_gather(ssm_terms.astype(jnp.bfloat16), 'exp')]
    psum x1 -> x0, waiting for transfers between devices: 58.9 us -> none  [body(): lax.psum(ssm_terms.astype(jnp.bfloat16), 'exp').astype(jnp.float32)]
    reduce_sum x0 -> x1, other arithmetic: none -> 4.91 us  [body(): jnp.sum(lax.all_gather(ssm_terms.astype(jnp.bfloat16), 'exp'), axis=0)]
where the time goes in v1:
time: 372 us; the launch traced here: 371 us
  waiting for transfers between devices  268 us (72%)
  matrix products  50.5 us (14%)
  starting transfers between devices  18.6 us (5%)
  between operations  13.5 us (4%)
  other arithmetic  10.2 us (3%)
  local copies, waits for them, and re-layouts  9.85 us (3%)
    all_gather x1, waiting for transfers between devices, body(): lax.all_gather(ssm_terms.astype(jnp.bfloat16), 'exp')  82.2 us
    all_gather x1, waiting for transfers between devices, body(): lax.all_gather(out_weight, 'ctx', axis=1, tiled=True)  54.2 us
    reduce_scatter x1, waiting for transfers between devices, body(): lax.psum_scatter(jnp.dot(hidden, down_weight[0], preferred_element_type=j...  35.4 us
    all_gather x1, waiting for transfers between devices, body(): normed_rows = lax.all_gather(picked, 'ctx', axis=0, tiled=True)  34.9 us
    ppermute x3, waiting for transfers between devices, passed_along(): return lax.ppermute(block, axis, route)  28.4 us
    dot_general x1, matrix products, body(): jnp.dot(hidden, down_weight[0], preferred_element_type=jnp.float32)  25.2 us
    all_gather x1, waiting for transfers between devices, body(): stream_full = lax.all_gather(stream_slice, 'exp', axis=1, tiled=True)  19.8 us
    dot_general x1, matrix products, body(): jnp.dot(normed_rows, gate_weight[0], preferred_element_type=jnp.float32)  16.7 us
  transfers between devices with their start and end apart: 9, of which 9 were waited for; matrix products, arithmetic and copies ran while one was open for 3% of the time, Pallas kernels for 0%

profile of v1, /device:TPU:0, one launch (start us, length us, event | category | flops | bytes accessed | tf_op | source)
XLA Modules:
  0.0 371.2 jit_solution(3621426297183494393)
XLA Ops:
  6.5 0.0 all-gather.6.cloned.1.call-start
  6.6 0.7 all-gather.6.cloned.1.call-update
  7.3 0.0 all-gather.12.cloned.1.call-start
  7.3 1.1 copy.60
  8.5 1.1 copy.61
  9.6 0.1 compare_select_fusion
  9.7 0.3 reduce_window_sum.22
  10.0 0.2 multiply_reduce_fusion.1
  10.2 0.1 exponential_multiply_fusion
  10.3 0.5 fusion.27
  10.9 42.7 %while.11 = (s32[]{:T(128)}, f32[16,64,128]{2,1,0:T(8,128)S(1)}, f32[16,1]{0,1:T(1,128)S(1)}, f32[16,64,128]{2,1,0:T(8,128)S(1)}, s32[]{:T(128)}, /*index=5*/s32[]{:T(128)}) while((s32[]{:T(128)}, f32[16,64,128]{2,1,0:T(8,128)S(1)}, f32[16,1]{0,1:T(1,128)S(1)}, f32[16,64,128]{2,1,0:T(8,128)S(1)}, s32[]{:T(128)}, ...), condition=%wide.region_2.3_spmd.clone, body=%wide.region_1.2_spmd.clone.sunk | while | flops 655363 | bytes 3145911 | solution.py:106
  10.9 0.1 fusion.72
  11.0 4.9 %collective-permute-start = (bf16[16,64,128]{2,1,0:T(8,128)(2,1)S(1)}, bf16[16,64,128]{2,1,0:T(8,128)(2,1)S(1)}, u32[]{:S(2)}, u32[]{:S(2)}) collective-permute-start(bf16[16,64,128]{2,1,0:T(8,128)(2,1)S(1)} %fusion.72), channel_id=1, source_target_pairs={{0,8},{8,16},{16,24},{1,9},{9,17},{17,25},{2,10},{10,18},{18,26},{... | collective-permute-start | bytes 786440 | tf_op jit(solution)/shard_map/while/body/eval_jaxpr/ppermute | solution.py:16
  15.9 5.5 %collective-permute-done = bf16[16,64,128]{2,1,0:T(8,128)(2,1)S(1)} collective-permute-done((bf16[16,64,128]{2,1,0:T(8,128)(2,1)S(1)}, bf16[16,64,128]{2,1,0:T(8,128)(2,1)S(1)}, u32[]{:S(2)}, u32[]{:S(2)}) %collective-permute-start) | collective-permute-done | bytes 262176 | tf_op jit(solution)/shard_map/while/body/eval_jaxpr/ppermute | solution.py:16
  21.5 0.1 fusion.72
  21.6 4.4 %collective-permute-start = (bf16[16,64,128]{2,1,0:T(8,128)(2,1)S(1)}, bf16[16,64,128]{2,1,0:T(8,128)(2,1)S(1)}, u32[]{:S(2)}, u32[]{:S(2)}) collective-permute-start(bf16[16,64,128]{2,1,0:T(8,128)(2,1)S(1)} %fusion.72), channel_id=1, source_target_pairs={{0,8},{8,16},{16,24},{1,9},{9,17},{17,25},{2,10},{10,18},{18,26},{... | collective-permute-start | bytes 786440 | tf_op jit(solution)/shard_map/while/body/eval_jaxpr/ppermute | solution.py:16
  26.0 11.6 %collective-permute-done = bf16[16,64,128]{2,1,0:T(8,128)(2,1)S(1)} collective-permute-done((bf16[16,64,128]{2,1,0:T(8,128)(2,1)S(1)}, bf16[16,64,128]{2,1,0:T(8,128)(2,1)S(1)}, u32[]{:S(2)}, u32[]{:S(2)}) %collective-permute-start) | collective-permute-done | bytes 262176 | tf_op jit(solution)/shard_map/while/body/eval_jaxpr/ppermute | solution.py:16
  37.6 0.1 fusion.72
  37.8 4.4 %collective-permute-start = (bf16[16,64,128]{2,1,0:T(8,128)(2,1)S(1)}, bf16[16,64,128]{2,1,0:T(8,128)(2,1)S(1)}, u32[]{:S(2)}, u32[]{:S(2)}) collective-permute-start(bf16[16,64,128]{2,1,0:T(8,128)(2,1)S(1)} %fusion.72), channel_id=1, source_target_pairs={{0,8},{8,16},{16,24},{1,9},{9,17},{17,25},{2,10},{10,18},{18,26},{... | collective-permute-start | bytes 786440 | tf_op jit(solution)/shard_map/while/body/eval_jaxpr/ppermute | solution.py:16
  42.2 11.3 %collective-permute-done = bf16[16,64,128]{2,1,0:T(8,128)(2,1)S(1)} collective-permute-done((bf16[16,64,128]{2,1,0:T(8,128)(2,1)S(1)}, bf16[16,64,128]{2,1,0:T(8,128)(2,1)S(1)}, u32[]{:S(2)}, u32[]{:S(2)}) %collective-permute-start) | collective-permute-done | bytes 262176 | tf_op jit(solution)/shard_map/while/body/eval_jaxpr/ppermute | solution.py:16
  53.6 0.4 fusion.26
  54.0 0.1 fusion.61
  54.1 0.6 fusion.29
  54.7 0.2 copy.62
  54.9 0.2 fusion.60
  55.1 0.4 mul.209
  55.5 0.2 reduce_sum.57
  55.8 0.2 mul.210
  56.0 0.1 copy.71
  56.1 54.2 %all-gather.6.cloned.1.call-done = bf16[1024,4096]{1,0:T(8,128)(2,1)} async-done(((bf16[1024,1024]{1,0:T(8,128)(2,1)}), bf16[1024,4096]{1,0:T(8,128)(2,1)}) %all-gather.6.cloned.1.call-update) | async-done | bytes 8388624 | tf_op jit(solution)/shard_map/all_gather | solution.py:123
  110.3 5.8 %convolution_convert_fusion = bf16[128,4096]{1,0:T(8,128)(2,1)} fusion(bf16[1024,4096]{1,0:T(8,128)(2,1)} %all-gather.6.cloned.1.call-done, f32[128,1024]{1,0:T(8,128)S(1)} %bitcast.101, f32[1024]{0:T(1024)S(1)} %copy-done.10, f32[128,1024]{1,0:T(8,128)S(1)} %copy.62, bf16[128,1024]{1,0:T(8,128)(2,1)S(1)} %copy-done.3), kind=kOutput, calls=%fused_computation.12 | convolution fusion | flops 1075445760 | bytes 10752000 | tf_op jit(solution)/shard_map/dot_general | solution.py:121
  116.1 0.0 all-gather.12.cloned.1.call-update
  116.2 0.0 all-gather.8.cloned.1.call-start
  116.2 82.2 %all-gather.12.cloned.1.call-done = bf16[1024,4096]{1,0:T(8,128)(2,1)} async-done(((bf16[128,4096]{1,0:T(8,128)(2,1)}), bf16[1024,4096]{1,0:T(8,128)(2,1)}) %all-gather.12.cloned.1.call-update) | async-done | bytes 8388624 | tf_op jit(solution)/shard_map/all_gather | solution.py:131
  198.4 4.9 %reduce_sum.58 = bf16[128,4096]{1,0:T(8,128)(2,1)S(1)} reduce(bf16[8,128,4096]{2,1,0:T(8,128)(2,1)} %bitcast.94, bf16[]{:T(256)} %constant.94.clone.1), dimensions={0}, to_apply=%region_4.5 | reduce | flops 3670016 | bytes 9437186 | tf_op jit(solution)/shard_map/reduce_sum | solution.py:131
  203.3 1.6 add_convert_fusion
  204.9 0.0 all-gather.8.cloned.1.call-update
  204.9 0.0 all-gather.10.cloned.1.call-start
  205.0 0.1 copy.65
  205.1 0.2 reduce_window_sum.23
  205.3 0.2 fusion.50
  205.6 0.2 select_reduce_fusion
  205.9 19.8 %all-gather.8.cloned.1.call-done = bf16[128,4096]{1,0:T(8,128)(2,1)} async-done(((bf16[128,512]{1,0:T(8,128)(2,1)}), bf16[128,4096]{1,0:T(8,128)(2,1)}) %all-gather.8.cloned.1.call-update) | async-done | bytes 1048592 | tf_op jit(solution)/shard_map/all_gather | solution.py:137
  225.7 1.3 concatenate.3
  227.1 0.9 gather_fusion
  227.9 0.3 fusion.32
  228.3 1.0 fusion.34
  229.3 0.0 all-gather.10.cloned.1.call-update
  229.3 0.2 reduce-scatter.2.cloned.1.call-start
  229.5 34.9 %all-gather.10.cloned.1.call-done = bf16[256,4096]{1,0:T(8,128)(2,1)} async-done(((bf16[64,4096]{1,0:T(8,128)(2,1)}), bf16[256,4096]{1,0:T(8,128)(2,1)}) %all-gather.10.cloned.1.call-update) | async-done | bytes 2097168 | tf_op jit(solution)/shard_map/all_gather | solution.py:143
  264.4 16.7 %fusion.6 = f32[256,3072]{1,0:T(8,128)} fusion(bf16[256,4096]{1,0:T(8,128)(2,1)} %all-gather.10.cloned.1.call-done, bf16[1,4096,3072]{2,1,0:T(8,128)(2,1)} %param.29), kind=kOutput, calls=%fused_computation.9 | convolution fusion | flops 6442450944 | bytes 30408704 | tf_op jit(solution)/shard_map/dot_general | solution.py:144
  281.1 25.2 %fusion.8 = bf16[256,4096]{1,0:T(8,128)(2,1)} fusion(bf16[1,3072,4096]{2,1,0:T(8,128)(2,1)} %param.31, bf16[256,4096]{1,0:T(8,128)(2,1)S(1)} %copy-done.9, bf16[1,4096,3072]{2,1,0:T(8,128)(2,1)} %param.30, f32[256,3072]{1,0:T(8,128)} %fusion.6), kind=kOutput, calls=%fused_computation.11 | convolution fusion | flops 12890669056 | bytes 57671680 | tf_op jit(solution)/shard_map/dot_general | solution.py:148
  306.3 0.0 reduce-scatter.2.cloned.1.call-update
  306.3 35.4 %reduce-scatter.2.cloned.1.call-done = bf16[64,4096]{1,0:T(8,128)(2,1)} async-done(((bf16[256,4096]{1,0:T(8,128)(2,1)}), bf16[64,4096]{1,0:T(8,128)(2,1)}) %reduce-scatter.2.cloned.1.call-update) | async-done | bytes 524304 | tf_op jit(solution)/shard_map/reduce_scatter | solution.py:147
  341.7 1.9 copy.74
  343.6 4.6 %all-to-all-start = ((bf16[64,8,512]{2,0,1:T(8,128)(2,1)}), bf16[64,8,512]{2,0,1:T(8,128)(2,1)S(1)}, u32[]{:S(2)}, u32[]{:S(2)}) async-start(bf16[64,8,512]{2,0,1:T(8,128)(2,1)} %bitcast.91), calls=%async_computation.1 | async-start | bytes 1048576 | tf_op jit(solution)/shard_map/all_to_all | solution.py:153
  348.2 0.1 copy.66
  348.3 0.1 reshape.219
  348.5 1.9 gather_fusion.1
  350.5 0.1 reshape.222
  350.6 0.1 copy.67
  350.7 0.0 copy-done.8
  350.8 12.8 %all-to-all-done = bf16[64,8,512]{2,0,1:T(8,128)(2,1)S(1)} async-done(((bf16[64,8,512]{2,0,1:T(8,128)(2,1)}), bf16[64,8,512]{2,0,1:T(8,128)(2,1)S(1)}, u32[]{:S(2)}, u32[]{:S(2)}) %all-to-all-start) | async-done | bytes 524320 | tf_op jit(solution)/shard_map/all_to_all | solution.py:153
  363.6 1.1 fusion.31
  (48 shorter events, 0.4 us)
Async XLA Ops:
  6.5 47.1 %copy-start = (bf16[128,128]{1,0:T(8,128)(2,1)S(1)}, bf16[128,128]{1,0:T(8,128)(2,1)}, u32[]{:S(2)}) copy-start(bf16[128,128]{1,0:T(8,128)(2,1)} %param.22) | copy-start | bytes 98308
  6.5 3.0 copy-start.4
  6.5 3.0 copy-start.11
  6.5 3.1 copy-start.5
  6.5 103.8 %all-gather.6.cloned.1.call-start = ((), (), s32[]{:S(2)}) async-start(), calls=%async_computation.2 | async-start | bytes 10485760 | tf_op jit(solution)/shard_map/all_gather | solution.py:123
  7.3 191.1 %all-gather.12.cloned.1.call-start = ((), (), s32[]{:S(2)}) async-start(), calls=%async_computation.6 | async-start | bytes 9437184 | tf_op jit(solution)/shard_map/all_gather | solution.py:131
  10.8 43.3 %copy-start.12 = (f32[16]{0:T(128)S(1)}, f32[16]{0:T(128)}, u32[]{:S(2)}) copy-start(f32[16]{0:T(128)} %param.25) | copy-start | bytes 196
  11.0 10.4 %collective-permute-start = (bf16[16,64,128]{2,1,0:T(8,128)(2,1)S(1)}, bf16[16,64,128]{2,1,0:T(8,128)(2,1)S(1)}, u32[]{:S(2)}, u32[]{:S(2)}) collective-permute-start(bf16[16,64,128]{2,1,0:T(8,128)(2,1)S(1)} %fusion.72), channel_id=1, source_target_pairs={{0,8},{8,16},{16,24},{1,9},{9,17},{17,25},{2,10},{10,18},{18,26},{... | collective-permute-start | bytes 786440 | tf_op jit(solution)/shard_map/while/body/eval_jaxpr/ppermute | solution.py:16
  21.6 16.0 %collective-permute-start = (bf16[16,64,128]{2,1,0:T(8,128)(2,1)S(1)}, bf16[16,64,128]{2,1,0:T(8,128)(2,1)S(1)}, u32[]{:S(2)}, u32[]{:S(2)}) collective-permute-start(bf16[16,64,128]{2,1,0:T(8,128)(2,1)S(1)} %fusion.72), channel_id=1, source_target_pairs={{0,8},{8,16},{16,24},{1,9},{9,17},{17,25},{2,10},{10,18},{18,26},{... | collective-permute-start | bytes 786440 | tf_op jit(solution)/shard_map/while/body/eval_jaxpr/ppermute | solution.py:16
  37.8 15.7 %collective-permute-start = (bf16[16,64,128]{2,1,0:T(8,128)(2,1)S(1)}, bf16[16,64,128]{2,1,0:T(8,128)(2,1)S(1)}, u32[]{:S(2)}, u32[]{:S(2)}) collective-permute-start(bf16[16,64,128]{2,1,0:T(8,128)(2,1)S(1)} %fusion.72), channel_id=1, source_target_pairs={{0,8},{8,16},{16,24},{1,9},{9,17},{17,25},{2,10},{10,18},{18,26},{... | collective-permute-start | bytes 786440 | tf_op jit(solution)/shard_map/while/body/eval_jaxpr/ppermute | solution.py:16
  53.6 1.3 copy-start.3
  54.7 55.6 %copy-start.10 = (f32[1024]{0:T(1024)S(1)}, f32[1024]{0:T(1024)}, u32[]{:S(2)}) copy-start(f32[1024]{0:T(1024)} %param.26) | copy-start | bytes 12292
  116.2 109.6 %all-gather.8.cloned.1.call-start = ((), (), s32[]{:S(2)}) async-start(), calls=%async_computation.3 | async-start | bytes 1179648 | tf_op jit(solution)/shard_map/all_gather | solution.py:137
  198.4 6.6 %copy-start.7 = (s32[128,2]{0,1:T(2,128)S(1)}, s32[128,2]{0,1:T(2,128)}, u32[]{:S(2)}) copy-start(s32[128,2]{0,1:T(2,128)} %param.32) | copy-start | bytes 3076
  204.9 59.5 %all-gather.10.cloned.1.call-start = ((), (), s32[]{:S(2)}) async-start(), calls=%async_computation.4 | async-start | bytes 2621440 | tf_op jit(solution)/shard_map/all_gather | solution.py:143
  227.0 1.2 copy-start.6
  229.3 112.4 %reduce-scatter.2.cloned.1.call-start = ((), (), s32[]{:S(2)}) async-start(), calls=%async_computation.5 | async-start | bytes 2621440 | tf_op jit(solution)/shard_map/reduce_scatter | solution.py:147
  264.4 16.7 %copy-start.9 = (bf16[256,4096]{1,0:T(8,128)(2,1)S(1)}, bf16[256,4096]{1,0:T(8,128)(2,1)}, u32[]{:S(2)}) copy-start(bf16[256,4096]{1,0:T(8,128)(2,1)} %all-gather.10.cloned.1.call-done) | copy-start | bytes 6291460
  343.6 20.0 %all-to-all-start = ((bf16[64,8,512]{2,0,1:T(8,128)(2,1)}), bf16[64,8,512]{2,0,1:T(8,128)(2,1)S(1)}, u32[]{:S(2)}, u32[]{:S(2)}) async-start(bf16[64,8,512]{2,0,1:T(8,128)(2,1)} %bitcast.91), calls=%async_computation.1 | async-start | bytes 1048576 | tf_op jit(solution)/shard_map/all_to_all | solution.py:153
  348.5 2.2 copy-start.8
  348.5 15.1 %copy-start.2 = (bf16[128,512]{1,0:T(8,128)(2,1)S(1)}, bf16[128,512]{1,0:T(8,128)(2,1)}, u32[]{:S(2)}) copy-start(bf16[128,512]{1,0:T(8,128)(2,1)} %add_convert_fusion) | copy-start | bytes 393220
  348.5 16.2 %copy-start.1 = (bf16[128,128]{1,0:T(8,128)(2,1)S(1)}, bf16[128,128]{1,0:T(8,128)(2,1)}, u32[]{:S(2)}) copy-start(bf16[128,128]{1,0:T(8,128)(2,1)} %param.22) | copy-start | bytes 98308
Sparse Core Ops, SparseCore 0:
  9.2 101.0 all-gather.5
  116.3 82.0 all-gather.11
  205.0 20.6 all-gather.7
  229.4 34.9 all-gather.9
  306.5 35.1 reduce-scatter.1
